TPU v7x, 32 devices: a whole 2x2x4 slice. The times are simulated.
32 devices in a mesh: band: 2 (over x), tm: 2 (over core), inp: 8 (over z, y).
Axes of the slice: x: 2, y: 2, z: 4, core: 2. Of those that a mesh axis runs over, the one named last changes fastest.
Arguments:
- samples: int32 [1024, 131072], P('inp', ('band', 'tm')), parts along dimension 1, may hold values from -128 to 127
- flags: int32 [2048], P(('band', 'inp')), parts along dimension 0, may hold values 0 or 1
Outputs:
- visibilities: bfloat16 [256, 2, 1024, 1024], P(('band', 'inp'), None, None, 'tm'), parts along dimension 0
There are 2 independent parts, one for each index of `band`. A program takes and returns all parts, laid end to end along the dimension named above; each array names one. Nothing has to cross between parts.
Inputs may be any that keep to these rules, and one draw needn't show every extreme that they name: `samples`: whole numbers.
All inputs are finite; a program needn't handle non-finite values. No bound on the sum of `flags` on one device may be relied on, other than what follows from the above.
Results may differ from a plain program's by a relative error of at most 0.0056.
Values may be sent and summed in bfloat16 or wider, within the bound.
A program may use at most 128 MiB of HBM per device.

v0:
```python
import math

import jax
import jax.numpy as jnp
from jax import lax
from jax.sharding import PartitionSpec as P

NFFT = 1024
TAPS = 4
CH_FIRST = 384
CH = 128


def passed_along(value, axis, by):
    length = lax.axis_size(axis)
    pairs = [(i, i + by) for i in range(length) if 0 <= i + by < length]
    return lax.ppermute(value, axis, pairs)


def window_table():
    positions = jnp.arange(TAPS * NFFT, dtype=jnp.float32) + 0.5
    shaped = jnp.sinc((positions - TAPS * NFFT / 2) / NFFT)
    taper = 0.5 - 0.5 * jnp.cos(2 * math.pi * positions / (TAPS * NFFT))
    return (shaped * taper).reshape(TAPS, NFFT)


def transform_table():
    sample_idx = jnp.arange(NFFT, dtype=jnp.int32)
    chan_idx = CH_FIRST + jnp.arange(CH, dtype=jnp.int32)
    angles = (sample_idx[:, None] * chan_idx[None, :] % NFFT).astype(jnp.float32) * (
        2 * math.pi / NFFT
    )
    both = jnp.stack([jnp.cos(angles), -jnp.sin(angles)], axis=1) / math.sqrt(NFFT)
    return both.reshape(NFFT, 2 * CH)


def filter_bank(extended, window, frames):
    summed = jnp.zeros((extended.shape[0], frames, NFFT), jnp.float32)
    for tap_index in range(TAPS):
        begin = TAPS - 1 - tap_index
        summed = summed + window[tap_index] * extended[:, begin : begin + frames]
    return summed


def transform(filtered, table):
    rows, frames, width = filtered.shape
    out = jnp.dot(
        filtered.reshape(rows * frames, width),
        table,
        precision=lax.Precision.HIGHEST,
        preferred_element_type=jnp.float32,
    )
    return out.reshape(rows, frames, 2, CH)


def correlate(left_side, right_side):
    chans, frames, _, row_count = left_side.shape
    depth = 2 * frames
    real_rows = left_side.reshape(chans, depth, row_count)
    imag_rows = jnp.stack([left_side[:, :, 1], -left_side[:, :, 0]], axis=2).reshape(
        chans, depth, row_count
    )
    left_both = jnp.stack([real_rows, imag_rows], axis=1)
    right_rows = right_side.reshape(chans, depth, right_side.shape[3])
    out = jnp.einsum("crka,ckb->crab", left_both, right_rows, preferred_element_type=jnp.float32)
    return out.astype(jnp.bfloat16)


def local(samples, flags):
    row_count = samples.shape[0]
    frames_dev = samples.shape[1] // NFFT
    window = window_table()
    table = transform_table()
    voltage = (
        (samples.astype(jnp.float32) / 128.0)
        .astype(jnp.bfloat16)
        .reshape(row_count, frames_dev, NFFT)
    )
    local_volts = voltage.astype(jnp.float32)
    leading = jnp.zeros((row_count, TAPS - 1, NFFT), jnp.float32)
    spectra = transform(
        filter_bank(jnp.concatenate([leading, local_volts], axis=1), window, frames_dev), table
    )
    weight = flags.astype(jnp.float32)[:, None, None, None]
    received = passed_along(voltage[:, frames_dev - (TAPS - 1) :], "tm", 1)
    source = jnp.concatenate([received.astype(jnp.float32), leading], axis=1)
    tail_part = transform(filter_bank(source, window, TAPS - 1), table)
    spectra = spectra.at[:, : TAPS - 1].add(tail_part)
    channels = (spectra * weight).astype(jnp.bfloat16).transpose(3, 1, 2, 0)
    timed = lax.all_gather(channels, "tm", axis=1, tiled=True)
    left_all = lax.all_to_all(timed, "inp", split_axis=0, concat_axis=3, tiled=True)
    total_inputs = left_all.shape[3]
    half_width = total_inputs // lax.axis_size("tm")
    right_side = lax.dynamic_slice_in_dim(
        left_all, lax.axis_index("tm") * half_width, half_width, 3
    )
    return correlate(left_all, right_side)


def solution(mesh):
    return jax.shard_map(
        local,
        mesh=mesh,
        in_specs=(P("inp", ("band", "tm")), P(("band", "inp"))),
        out_specs=P(("band", "inp"), None, None, "tm"),
        check_vma=False,
    )
```

profile of v0, /device:TPU:0, one launch (start us, length us, event | category | flops | bytes accessed | tf_op | source)
XLA Modules:
  0.0 252.5 jit_solution(2288556194103495680)
XLA Ops:
  6.5 6.6 %multiply_convert_fusion = bf16[128,32768]{1,0:T(8,128)(2,1)S(1)} fusion(s32[128,32768]{1,0:T(8,128)} %param.4), kind=kLoop, calls=%fused_computation.13 | loop fusion | flops 12582912 | bytes 25165824 | tf_op jit(solution)/shard_map/convert_element_type | solution.py:76
  13.1 7.1 %copy_bitcast_fusion = (bf16[128,32,1024]{2,0,1:T(8,128)(2,1)S(1)}, f32[128,32,1024]{2,0,1:T(8,128)}) fusion(bf16[16,32,8,1024]{3,2,1,0:T(8,128)(2,1)S(1)} %bitcast.46), kind=kLoop, calls=%fused_computation.14 | loop fusion | flops 4194304 | bytes 33554432 | tf_op jit(solution)/shard_map/reshape | solution.py:77
  20.3 2.4 collective-permute-start
  22.9 2.1 fusion.52
  25.0 23.9 %fusion.5 = f32[128,32,2,128]{3,0,2,1:T(8,128)S(1)} fusion(f32[128,32,1024]{2,0,1:T(8,128)} %get-tuple-element.18, f32[1024]{0:T(1024)S(1)} %get-tuple-element.22, f32[1024]{0:T(1024)S(1)} %get-tuple-element.23, f32[1024]{0:T(1024)S(1)} %get-tuple-element.24, f32[1024]{0:T(1024)S(1)} %get-tuple-element.25, f32[1024,1,128]{0,2,1:T(8,128)S(1)} %get-tuple-element.27, ...), kind=kOutput, calls=%fused_computation.9 | convolution fusion | flops 12914786304 | bytes 22036480 | tf_op jit(solution)/shard_map/dot_general | solution.py:47
  49.2 1.7 fusion.34
  51.5 2.9 %copy.18 = bf16[128,32,2,128]{3,0,2,1:T(8,128)(2,1)} copy(bf16[128,32,2,128]{0,3,2,1:T(8,128)(2,1)S(1)} %fusion.19) | data formatting | bytes 4194304 | tf_op jit(solution)/shard_map/transpose | solution.py:89
  54.4 15.9 %all-gather.2.cloned.1.call-done = bf16[128,64,2,128]{3,0,2,1:T(8,128)(2,1)} async-done(((bf16[128,32,2,128]{3,0,2,1:T(8,128)(2,1)}), bf16[128,64,2,128]{3,0,2,1:T(8,128)(2,1)}) %all-gather.2.cloned.1.call-update) | async-done | bytes 4194320 | tf_op jit(solution)/shard_map/all_gather | solution.py:90
  70.3 8.5 %copy.19 = bf16[128,64,2,128]{3,2,1,0:T(2,128)(2,1)} copy(bf16[128,64,2,128]{3,0,2,1:T(8,128)(2,1)} %all-gather.2.cloned.1.call-done) | data formatting | bytes 8388608 | tf_op jit(solution)/shard_map/all_gather | solution.py:90
  78.9 5.8 %all-to-all-start = ((bf16[128,64,2,128]{3,2,1,0:T(2,128)(2,1)}), bf16[128,64,2,128]{3,2,1,0:T(2,128)(2,1)}, u32[]{:S(2)}, u32[]{:S(2)}) async-start(bf16[128,64,2,128]{3,2,1,0:T(2,128)(2,1)} %copy.19), calls=%async_computation | async-start | bytes 8388608 | tf_op jit(solution)/shard_map/all_to_all | solution.py:91
  84.6 93.7 %all-to-all-done = bf16[128,64,2,128]{3,2,1,0:T(2,128)(2,1)} async-done(((bf16[128,64,2,128]{3,2,1,0:T(2,128)(2,1)}), bf16[128,64,2,128]{3,2,1,0:T(2,128)(2,1)}, u32[]{:S(2)}, u32[]{:S(2)}) %all-to-all-start) | async-done | bytes 4194336 | tf_op jit(solution)/shard_map/all_to_all | solution.py:91
  178.4 3.4 %copy.20 = bf16[128,64,2,128]{3,1,2,0:T(8,128)(2,1)S(1)} copy(bf16[128,64,2,128]{3,2,1,0:T(2,128)(2,1)} %all-to-all-done) | data formatting | bytes 8388608 | tf_op jit(solution)/shard_map/all_to_all | solution.py:91
  181.8 2.0 copy-done
  183.8 5.6 %copy.21 = bf16[16,64,2,8,128]{4,3,2,1,0:T(8,128)(2,1)} copy(bf16[16,64,2,8,128]{4,1,2,0,3:T(8,128)(2,1)S(1)} %bitcast.44) | data formatting | bytes 8388608 | tf_op jit(solution)/shard_map/all_to_all | solution.py:91
  189.4 7.4 %stack_reshape.6 = bf16[16,1,128,1024]{3,2,0,1:T(8,128)(2,1)} reshape(bf16[16,64,2,8,128]{4,3,2,1,0:T(8,128)(2,1)} %copy.21) | data formatting | bytes 8388608 | tf_op jit(solution)/shard_map/stack;reshape | solution.py:63
  196.8 6.4 %copy.24 = bf16[16,1,128,1024]{2,3,1,0:T(8,128)(2,1)} copy(bf16[16,1,128,1024]{3,2,0,1:T(8,128)(2,1)} %stack_reshape.6) | data formatting | bytes 8388608 | tf_op jit(solution)/shard_map/stack;reshape | solution.py:63
  203.2 3.3 %copy.36 = bf16[8,16,2,8,8,128]{5,4,0,3,2,1:T(8,128)(2,1)S(1)} copy(bf16[8,16,2,8,8,128]{5,4,3,2,1,0:T(8,128)(2,1)} %bitcast.45) | data formatting | bytes 8388608 | tf_op jit(solution)/shard_map/all_to_all | solution.py:91
  206.5 2.3 fusion.90
  209.1 2.2 copy.26
  211.3 2.3 reshape.177
  213.5 2.6 %pad_maximum_fusion = bf16[16,64,2,1024]{3,1,2,0:T(8,128)(2,1)S(1)} fusion(bf16[16,64,1,1024]{3,1,2,0:T(8,128)(2,1)} %get-tuple-element.20, bf16[16,64,1,1024]{3,1,2,0:T(8,128)(2,1)} %get-tuple-element.19), kind=kLoop, calls=%fused_computation.23 | loop fusion | flops 2097152 | bytes 8388608 | tf_op jit(solution)/shard_map/stack | solution.py:60
  216.1 4.3 %copy.23 = bf16[16,64,2,1024]{3,0,2,1:T(8,128)(2,1)} copy(bf16[16,64,2,1024]{3,1,2,0:T(8,128)(2,1)S(1)} %pad_maximum_fusion) | data formatting | bytes 8388608 | tf_op jit(solution)/shard_map/stack | solution.py:60
  220.5 6.7 %copy.25 = bf16[16,1,128,1024]{2,3,1,0:T(8,128)(2,1)} copy(bf16[16,1,128,1024]{3,0,2,1:T(8,128)(2,1)} %bitcast.49) | data formatting | bytes 8388608 | tf_op jit(solution)/shard_map/stack;reshape | solution.py:63
  227.2 18.4 %convolution_convert_fusion = bf16[16,2,1024,512]{3,2,1,0:T(8,128)(2,1)} fusion(bf16[16,1,128,1024]{2,3,1,0:T(8,128)(2,1)} %copy.25, bf16[16,1,128,1024]{2,3,1,0:T(8,128)(2,1)} %copy.24, bf16[16,128,512,1]{2,1,0,3:T(8,128)(2,1)S(1)} %copy-done.1), kind=kOutput, calls=%fused_computation | convolution fusion | flops 4315938816 | bytes 44040192 | tf_op jit(solution)/shard_map/crka,ckb->crab/dot_general | solution.py:65
  (16 shorter events, 1.2 us)
Async XLA Ops:
  6.5 63.8 %all-gather.2.cloned.1.call-start = ((), (), s32[]{:S(2)}) async-start(), calls=%async_computation.1 | async-start | bytes 6291456 | tf_op jit(solution)/shard_map/all_gather | solution.py:90
  20.3 28.6 %collective-permute-start = (bf16[128,3,1024]{2,0,1:T(8,128)(2,1)S(1)}, bf16[128,3,1024]{2,0,1:T(8,128)(2,1)S(1)}, u32[]{:S(2)}, u32[]{:S(2)}) collective-permute-start(bf16[128,3,1024]{2,0,1:T(8,128)(2,1)S(1)} %slice.99), channel_id=1, source_target_pairs={{0,8},{1,9},{2,10},{3,11},{4,12},{5,13},{6,14},{7,15},{16,24},{17,... | collective-permute-start | bytes 2359304 | tf_op jit(solution)/shard_map/ppermute | solution.py:17
  25.0 23.9 %copy-start.2 = (s32[128]{0:T(128)S(1)}, s32[128]{0:T(128)}, u32[]{:S(2)}) copy-start(s32[128]{0:T(128)} %param.5) | copy-start | bytes 1540
  78.9 99.5 %all-to-all-start = ((bf16[128,64,2,128]{3,2,1,0:T(2,128)(2,1)}), bf16[128,64,2,128]{3,2,1,0:T(2,128)(2,1)}, u32[]{:S(2)}, u32[]{:S(2)}) async-start(bf16[128,64,2,128]{3,2,1,0:T(2,128)(2,1)} %copy.19), calls=%async_computation | async-start | bytes 8388608 | tf_op jit(solution)/shard_map/all_to_all | solution.py:91
  181.8 2.0 copy-start
  220.5 6.7 %copy-start.1 = (bf16[16,128,512,1]{2,1,0,3:T(8,128)(2,1)S(1)}, bf16[16,128,512,1]{2,1,0,3:T(8,128)(2,1)}, u32[]{:S(2)}) copy-start(bf16[16,128,512,1]{2,1,0,3:T(8,128)(2,1)} %reshape.177) | copy-start | bytes 6291460
Sparse Core Ops, SparseCore 0:
  54.5 15.7 all-gather.1
where the time goes:
time: 253 us
  waiting for transfers between devices  110 us (43%)
  local copies, waits for them, and re-layouts  55.4 us (22%)
  matrix products  44.1 us (17%)
  other arithmetic  21.6 us (9%)
  between operations  13.5 us (5%)
  starting transfers between devices  8.18 us (3%)
    all_to_all x1, waiting for transfers between devices, local(): lax.all_to_all(timed, 'inp', split_axis=0, concat_axis=3, tiled=True)  93.7 us
    dot_general x2, matrix products, transform(): jnp.dot(filtered.reshape(rows * frames, width), table, precision=lax.Prec...  25.7 us
    another operation x3, local copies, waits for them, and re-layouts, correlate(): left_both = jnp.stack([real_rows, imag_rows], axis=1)  20.5 us
    dot_general x1, matrix products, correlate(): jnp.einsum('crka,ckb->crab', left_both, right_rows, preferred_element_typ...  18.4 us
    all_gather x1, waiting for transfers between devices, local(): timed = lax.all_gather(channels, 'tm', axis=1, tiled=True)  15.9 us
    all_to_all x3, local copies, waits for them, and re-layouts, local(): lax.all_to_all(timed, 'inp', split_axis=0, concat_axis=3, tiled=True)  12.3 us
    all_gather x1, local copies, waits for them, and re-layouts, local(): timed = lax.all_gather(channels, 'tm', axis=1, tiled=True)  8.51 us
    reshape x1, other arithmetic, local(): voltage = (samples.astype(jnp.float32) / 128.0).astype(jnp.bfloat16).resh...  7.14 us
  transfers between devices with their start and end apart: 3, of which 2 were waited for; matrix products, arithmetic and copies ran while one was open for 10% of the time, Pallas kernels for 0%

commit v1 on v0

v1 whole, which is shorter than its diff:
```python
import functools
import math

import jax
import jax.numpy as jnp
import ml_dtypes
import numpy as np
from jax import lax
from jax.experimental import pallas as pl
from jax.experimental.pallas import tpu as pltpu
from jax.sharding import PartitionSpec as P

NFFT = 1024
TAPS = 4
CH_FIRST = 384
CH = 128
CHUNK = 16
MESH = pl.DeviceIdType.MESH


def window_table():
    positions = np.arange(TAPS * NFFT, dtype=np.float64) + 0.5
    shaped = np.sinc((positions - TAPS * NFFT / 2) / NFFT)
    taper = 0.5 - 0.5 * np.cos(2 * math.pi * positions / (TAPS * NFFT))
    return (shaped * taper).reshape(TAPS, NFFT)


def transform_table():
    sample_idx = np.arange(NFFT)
    chan_idx = CH_FIRST + np.arange(CH)
    angles = (chan_idx[:, None] * sample_idx[None, :] % NFFT) * (2 * math.pi / NFFT)
    both = np.stack([np.cos(angles), -np.sin(angles)], axis=1) / math.sqrt(NFFT)
    return both.reshape(2 * CH, NFFT)


def split_table():
    table = transform_table().astype(np.float32)
    high = table.astype(ml_dtypes.bfloat16)
    low = (table - high.astype(np.float32)).astype(ml_dtypes.bfloat16)
    return np.concatenate([high, low], axis=0)


def spread_kernel(
    peers, frames, samples, flags, window, table, gathered,
    volts, halo_out, halo_in, high, low, spectra, ready,
    load_sem, halo_sems, send_sem, recv_sem, fwd_send, fwd_recv, own_sem,
):
    rows = samples.shape[0]
    lead = TAPS - 1
    chunks = frames // CHUNK
    me = lax.axis_index("inp")
    core = lax.axis_index("tm")
    other = 1 - core
    mine = ready.shape[1] // peers
    offsets = sorted(range(1, peers), key=lambda d: (abs(d - peers / 2), d))

    def load(frame):
        return pltpu.make_async_copy(
            samples.at[:, pl.ds(pl.multiple_of(frame * NFFT, NFFT), NFFT)],
            volts.at[frame + lead],
            load_sem.at[frame],
        )

    order = list(range(frames - lead, frames))
    for chunk in reversed(range(chunks)):
        begin = max(0, chunk * CHUNK - lead)
        order += [f for f in range(begin, (chunk + 1) * CHUNK) if f not in order]
    for frame in order:
        load(frame).start()

    barrier = pltpu.get_barrier_semaphore()
    for d in offsets:
        pl.semaphore_signal(
            barrier, inc=1, device_id={"inp": lax.rem(me + d, peers)}, device_id_type=MESH
        )
    pl.semaphore_signal(barrier, inc=1, device_id={"tm": other}, device_id_type=MESH)
    pl.semaphore_wait(barrier, peers)

    halo = pltpu.make_async_remote_copy(
        src_ref=halo_out, dst_ref=halo_in, send_sem=halo_sems.at[0], recv_sem=halo_sems.at[1],
        device_id={"tm": other}, device_id_type=MESH,
    )
    for j in range(lead):
        load(frames - lead + j).wait()
        halo_out[j] = volts[frames + j].astype(jnp.float32).astype(jnp.bfloat16)
    halo.start()

    def filter_pair(first):
        def row_group(g, carry):
            at = pl.ds(pl.multiple_of(g * 16, 16), 16)
            for part in range(NFFT // 256):
                cols = slice(part * 256, (part + 1) * 256)
                values = [
                    volts[first + j, at, cols].astype(jnp.float32) for j in range(TAPS + 1)
                ]
                taps = [
                    jnp.broadcast_to(window[k : k + 1, cols], (16, 256)) for k in range(TAPS)
                ]
                for j in range(2):
                    total = taps[0] * values[lead + j]
                    for k in range(1, TAPS):
                        total = total + taps[k] * values[lead + j - k]
                    top = total.astype(jnp.bfloat16)
                    dest = pl.ds(pl.multiple_of(j * rows + g * 16, 16), 16)
                    high[dest, cols] = top
                    low[dest, cols] = (total - top.astype(jnp.float32)).astype(jnp.bfloat16)
            return carry

        lax.fori_loop(0, rows // 16, row_group, 0)

    dims = (((1,), (1,)), ((), ()))

    def compute(chunk):
        def pair(q, carry):
            first = chunk * CHUNK + 2 * q
            filter_pair(first)
            both = lax.dot_general(
                table[...], high[...], dims, preferred_element_type=jnp.float32
            )
            rest = lax.dot_general(
                table[: 2 * CH], low[...], dims, preferred_element_type=jnp.float32
            )
            total = both[: 2 * CH] + (both[2 * CH :] + rest)
            good = flags[0:1, :]
            for j in range(2):
                spectra[pl.ds(pl.multiple_of((2 * q + j) * 2 * CH, 2 * CH), 2 * CH), :] = (
                    total[:, j * rows : (j + 1) * rows] * good
                )
            return carry

        lax.fori_loop(0, CHUNK // 2, pair, 0)

        def regroup(step, carry):
            for u in range(8):
                r = step * 8 + u
                ready[chunk, r] = spectra[pl.ds(r, CHUNK, stride=2 * CH), :].astype(
                    jnp.bfloat16
                )
            return carry

        lax.fori_loop(0, 2 * CH // 8, regroup, 0)

    def to_peer(chunk, d):
        dest = lax.rem(me + d, peers)
        return pltpu.make_async_remote_copy(
            src_ref=ready.at[chunk, pl.ds(dest * mine, mine)],
            dst_ref=gathered.at[me, core, chunk],
            send_sem=send_sem.at[chunk, d], recv_sem=recv_sem.at[chunk, d],
            device_id={"inp": dest}, device_id_type=MESH,
        )

    def own_local(chunk):
        return pltpu.make_async_copy(
            ready.at[chunk, pl.ds(me * mine, mine)], gathered.at[me, core, chunk],
            own_sem.at[chunk],
        )

    def own_other(chunk):
        return pltpu.make_async_remote_copy(
            src_ref=ready.at[chunk, pl.ds(me * mine, mine)],
            dst_ref=gathered.at[me, core, chunk],
            send_sem=fwd_send.at[chunk, 0], recv_sem=fwd_recv.at[chunk, 0],
            device_id={"tm": other}, device_id_type=MESH,
        )

    def forward(chunk, d):
        src = lax.rem(me + peers - d, peers)
        block = gathered.at[src, core, chunk]
        return pltpu.make_async_remote_copy(
            src_ref=block, dst_ref=block,
            send_sem=fwd_send.at[chunk, d], recv_sem=fwd_recv.at[chunk, d],
            device_id={"tm": other}, device_id_type=MESH,
        )

    waited = set(range(frames - lead, frames))
    for chunk in reversed(range(chunks)):
        for f in range(max(0, chunk * CHUNK - lead), (chunk + 1) * CHUNK):
            if f not in waited:
                waited.add(f)
                load(f).wait()
        if chunk == 0:
            halo.wait()
            scale = core.astype(jnp.float32)
            for j in range(lead):
                volts[j] = (halo_in[j].astype(jnp.float32) * scale).astype(jnp.int32)
        compute(chunk)
        for d in offsets:
            to_peer(chunk, d).start()
        own_local(chunk).start()
        own_other(chunk).start()

    for chunk in reversed(range(chunks)):
        for d in offsets:
            to_peer(chunk, d).wait_recv()
            forward(chunk, d).start()
    for chunk in reversed(range(chunks)):
        own_local(chunk).wait()
        own_other(chunk).wait()
        for d in offsets:
            to_peer(chunk, d).wait_send()
            forward(chunk, d).wait()


def spread(samples, flags, peers):
    rows, width = samples.shape
    frames = width // NFFT
    chunks = frames // CHUNK
    lead = TAPS - 1
    window = jnp.asarray((window_table() / 128.0).astype(np.float32))
    table = jnp.asarray(split_table())
    good = jnp.broadcast_to(flags.astype(jnp.float32)[None, :], (8, rows))
    vmem = pl.BlockSpec(memory_space=pltpu.VMEM)
    anywhere = pl.BlockSpec(memory_space=pl.ANY)
    return pl.pallas_call(
        functools.partial(spread_kernel, peers, frames),
        out_shape=jax.ShapeDtypeStruct(
            (peers, 2, chunks, 2 * CH // peers, CHUNK, rows), jnp.bfloat16
        ),
        in_specs=[anywhere, vmem, vmem, vmem],
        out_specs=anywhere,
        scratch_shapes=[
            pltpu.VMEM((frames + lead, rows, NFFT), jnp.int32),
            pltpu.VMEM((lead, rows, NFFT), jnp.bfloat16),
            pltpu.VMEM((lead, rows, NFFT), jnp.bfloat16),
            pltpu.VMEM((2 * rows, NFFT), jnp.bfloat16),
            pltpu.VMEM((2 * rows, NFFT), jnp.bfloat16),
            pltpu.VMEM((CHUNK * 2 * CH, rows), jnp.float32),
            pltpu.VMEM((chunks, 2 * CH, CHUNK, rows), jnp.bfloat16),
            pltpu.SemaphoreType.DMA((frames,)),
            pltpu.SemaphoreType.DMA((2,)),
            pltpu.SemaphoreType.DMA((chunks, peers)),
            pltpu.SemaphoreType.DMA((chunks, peers)),
            pltpu.SemaphoreType.DMA((chunks, peers)),
            pltpu.SemaphoreType.DMA((chunks, peers)),
            pltpu.SemaphoreType.DMA((chunks,)),
        ],
        compiler_params=pltpu.CompilerParams(
            collective_id=0, has_side_effects=True, vmem_limit_bytes=48 << 20
        ),
        name="filter_transform_spread",
    )(samples, good, window, table)


def correlate_kernel(block, out, left, right):
    peers, cores, chunks, _, length, rows = block.shape
    half = peers // 2
    core = lax.axis_index("tm")
    width = length * 2
    for src in range(peers):
        cols = slice(src * rows, (src + 1) * rows)
        for t in range(cores):
            for k in range(chunks):
                at = (t * chunks + k) * width
                real, imag = block[src, t, k, 0], block[src, t, k, 1]
                left[0, at : at + length, cols] = real
                left[0, at + length : at + width, cols] = imag
                left[1, at : at + length, cols] = imag
                left[1, at + length : at + width, cols] = -real
    for s in range(half):
        cols = slice(s * rows, (s + 1) * rows)
        for t in range(cores):
            for k in range(chunks):
                at = (t * chunks + k) * width
                right[at : at + length, cols] = block[core * half + s, t, k, 0]
                right[at + length : at + width, cols] = block[core * half + s, t, k, 1]
    step = 256
    for r in range(2):
        for a in range(0, left.shape[2], step):
            out[0, r, a : a + step, :] = lax.dot_general(
                left[r, :, a : a + step], right[...], (((0,), (0,)), ((), ())),
                preferred_element_type=jnp.float32,
            ).astype(jnp.bfloat16)


def correlate_blocks(gathered):
    peers, cores, chunks, parts, length, rows = gathered.shape
    chans = parts // 2
    total = peers * rows
    depth = cores * chunks * 2 * length
    return pl.pallas_call(
        correlate_kernel,
        grid=(chans,),
        out_shape=jax.ShapeDtypeStruct((chans, 2, total, total // 2), jnp.bfloat16),
        in_specs=[
            pl.BlockSpec(
                (peers, cores, chunks, 2, length, rows), lambda c: (0, 0, 0, c, 0, 0)
            )
        ],
        out_specs=pl.BlockSpec((1, 2, total, total // 2), lambda c: (c, 0, 0, 0)),
        scratch_shapes=[
            pltpu.VMEM((2, depth, total), jnp.bfloat16),
            pltpu.VMEM((depth, total // 2), jnp.bfloat16),
        ],
        compiler_params=pltpu.CompilerParams(vmem_limit_bytes=48 << 20),
        name="correlate",
    )(gathered)


def filter_bank(extended, window, frames):
    summed = jnp.zeros((extended.shape[0], frames, NFFT), jnp.float32)
    for tap_index in range(TAPS):
        begin = TAPS - 1 - tap_index
        summed = summed + window[tap_index] * extended[:, begin : begin + frames]
    return summed


def general(samples, flags):
    rows = samples.shape[0]
    frames = samples.shape[1] // NFFT
    window = jnp.asarray(window_table().astype(np.float32))
    table = jnp.asarray(transform_table().astype(np.float32))
    voltage = (samples.astype(jnp.float32) / 128.0).astype(jnp.bfloat16)
    voltage = voltage.reshape(rows, frames, NFFT)
    received = lax.ppermute(voltage[:, frames - (TAPS - 1) :], "tm", [(0, 1)])
    extended = jnp.concatenate([received, voltage], axis=1).astype(jnp.float32)
    filtered = filter_bank(extended, window, frames)
    spectra = lax.dot_general(
        filtered.reshape(rows * frames, NFFT), table, (((1,), (1,)), ((), ())),
        precision=lax.Precision.HIGHEST, preferred_element_type=jnp.float32,
    ).reshape(rows, frames, CH, 2)
    weight = flags.astype(jnp.float32)[:, None, None, None]
    channels = (spectra * weight).astype(jnp.bfloat16).transpose(2, 1, 3, 0)
    spread_out = lax.all_to_all(channels, "inp", split_axis=0, concat_axis=3, tiled=True)
    left = lax.all_gather(spread_out, "tm", axis=1, tiled=True)
    chans, _, _, total = left.shape
    half = total // 2
    right = lax.dynamic_slice_in_dim(left, lax.axis_index("tm") * half, half, 3)
    turned = jnp.stack([left[:, :, 1], -left[:, :, 0]], axis=2)
    both = jnp.stack([left, turned], axis=1).reshape(chans, 2, -1, total)
    out = jnp.einsum(
        "crka,ckb->crab", both, right.reshape(chans, -1, half),
        preferred_element_type=jnp.float32,
    )
    return out.astype(jnp.bfloat16)


def solution(mesh):
    peers = mesh.shape["inp"]

    def local(samples, flags):
        rows, width = samples.shape
        fits = (
            rows == 128 and peers % 2 == 0 and mesh.shape["tm"] == 2
            and (width // NFFT) % CHUNK == 0 and 2 * CH % (2 * peers) == 0
        )
        if not fits:
            return general(samples, flags)
        return correlate_blocks(spread(samples, flags, peers))

    return jax.shard_map(
        local,
        mesh=mesh,
        in_specs=(P("inp", ("band", "tm")), P(("band", "inp"))),
        out_specs=P(("band", "inp"), None, None, "tm"),
        check_vma=False,
    )
```

time: 253 us -> 84.9 us (0.34)
  waiting for transfers between devices: 110 us -> 0 us
  Pallas kernels: 0 us -> 80.7 us
  local copies, waits for them, and re-layouts: 55.4 us -> 1.95 us
  matrix products: 44.1 us -> 0 us
  other arithmetic: 21.6 us -> 0.66 us
  between operations: 13.5 us -> 0.01 us
  starting transfers between devices: 8.18 us -> 0 us
    all_to_all x1 -> x0, waiting for transfers between devices: 93.7 us -> none  [local(): lax.all_to_all(timed, 'inp', split_axis=0, concat_axis=3, tiled=True)]
    pallas_call x0 -> x2, Pallas kernels: none -> 80.7 us  [the longest x1 62.8 us: spread(): pl.pallas_call(functools.partial(spread_kernel, peers, frames), out_shape...]
    dot_general x3 -> x0, matrix products: 44.1 us -> none  [the longest x2 25.7 us: transform(): jnp.dot(filtered.reshape(rows * frames, width), table, precision=lax.Prec...]
    another operation x4 -> x0, local copies, waits for them, and re-layouts: 24.9 us -> none  [the longest x3 20.5 us: correlate(): left_both = jnp.stack([real_rows, imag_rows], axis=1)]
    all_gather x1 -> x0, waiting for transfers between devices: 15.9 us -> none  [local(): timed = lax.all_gather(channels, 'tm', axis=1, tiled=True)]
    all_to_all x3 -> x0, local copies, waits for them, and re-layouts: 12.3 us -> none  [local(): lax.all_to_all(timed, 'inp', split_axis=0, concat_axis=3, tiled=True)]
    all_gather x1 -> x0, local copies, waits for them, and re-layouts: 8.51 us -> none  [local(): timed = lax.all_gather(channels, 'tm', axis=1, tiled=True)]
    reshape x1 -> x0, other arithmetic: 7.14 us -> none  [local(): voltage = (samples.astype(jnp.float32) / 128.0).astype(jnp.bfloat16).resh...]
  transfers between devices with their start and end apart: 3 -> 0, of which waited for: 2 -> 0; matrix products, arithmetic and copies ran while one was open for 10% -> 0% of each run, Pallas kernels for 0% -> 0%
where the time goes in v1:
time: 84.9 us; the launch traced here: 83.3 us
  Pallas kernels  80.7 us (95%)
  local copies, waits for them, and re-layouts  1.95 us (2%)
    pallas_call x1, Pallas kernels, spread(): pl.pallas_call(functools.partial(spread_kernel, peers, frames), out_shape...  62.8 us
    pallas_call x1, Pallas kernels, correlate_blocks(): pl.pallas_call(correlate_kernel, grid=(chans,), out_shape=jax.ShapeDtypeS...  17.9 us
    unnamed x4, local copies, waits for them, and re-layouts  1.94 us

profile of v1, /device:TPU:0, one launch (start us, length us, event | category | flops | bytes accessed | tf_op | source)
XLA Modules:
  0.0 83.3 jit_solution(1383264536569639969)
XLA Ops:
  0.0 0.7 convert_element_type.3
  0.7 0.0 copy-start
  0.7 1.2 %copy-done = bf16[512,1024]{1,0:T(8,128)(2,1)S(1)} copy-done((bf16[512,1024]{1,0:T(8,128)(2,1)S(1)}, bf16[512,1024]{1,0:T(8,128)(2,1)}, u32[]{:S(2)}) %copy-start) | copy-done | bytes 1048600
  1.9 0.0 copy-start.1
  1.9 0.7 copy-done.1
  2.6 62.8 %filter_transform_spread.1.block = bf16[8,2,2,32,16,128]{5,4,3,2,1,0:T(8,128)(2,1)S(1)} custom-call(s32[128,32768]{1,0:T(8,128)} %samples.1, f32[8,128]{1,0:T(8,128)S(1)} %broadcast_in_dim.2.flags, f32[4,1024]{1,0:T(4,128)S(1)} %copy-done.1, bf16[512,1024]{1,0:T(8,128)(2,1)S(1)} %copy-done), custom_call_target="tpu_custom_call" | custom-call | tf_op jit(solution)/shard_map/filter_transform_spread/pallas_call | solution.py:214
  65.4 17.9 %correlate.1 = bf16[16,2,1024,512]{3,2,1,0:T(8,128)(2,1)} custom-call(bf16[8,2,2,32,16,128]{5,4,3,2,1,0:T(8,128)(2,1)S(1)} %filter_transform_spread.1.block), custom_call_target="tpu_custom_call" | custom-call | tf_op jit(solution)/shard_map/correlate/pallas_call | solution.py:280
  (1 shorter events, 0.0 us)
Async XLA Ops:
  0.7 1.2 %copy-start = (bf16[512,1024]{1,0:T(8,128)(2,1)S(1)}, bf16[512,1024]{1,0:T(8,128)(2,1)}, u32[]{:S(2)}) copy-start(bf16[512,1024]{1,0:T(8,128)(2,1)} %constant.5.clone.table) | copy-start | bytes 3145732
  1.9 0.7 copy-start.1

commit v2 on v1

--- a/solution.py
+++ b/solution.py
@@ -14,7 +14,7 @@
 TAPS = 4
 CH_FIRST = 384
 CH = 128
-CHUNK = 16
+CHUNK = 8
 MESH = pl.DeviceIdType.MESH
 
 
@@ -41,9 +41,9 @@
 
 
 def spread_kernel(
-    peers, frames, samples, flags, window, table, gathered,
-    volts, halo_out, halo_in, high, low, spectra, ready,
-    load_sem, halo_sems, send_sem, recv_sem, fwd_send, fwd_recv, own_sem,
+    peers, frames, samples, flags_hbm, window_hbm, table_hbm, gathered,
+    volts, flags, window, table, halo_out, halo_in, high, low, spectra, ready,
+    load_sem, const_sem, halo_sems, send_sem, recv_sem, fwd_send, fwd_recv, own_sem,
 ):
     rows = samples.shape[0]
     lead = TAPS - 1
@@ -61,29 +61,39 @@
             load_sem.at[frame],
         )
 
-    order = list(range(frames - lead, frames))
+    def barrier_part(wait):
+        barrier = pltpu.get_barrier_semaphore()
+        if wait:
+            pl.semaphore_wait(barrier, peers)
+            return
+        for d in offsets:
+            pl.semaphore_signal(
+                barrier, inc=1, device_id={"inp": lax.rem(me + d, peers)}, device_id_type=MESH
+            )
+        pl.semaphore_signal(barrier, inc=1, device_id={"tm": other}, device_id_type=MESH)
+
+    constants = [
+        pltpu.make_async_copy(src, dst, const_sem.at[k])
+        for k, (src, dst) in enumerate(
+            [(window_hbm, window), (flags_hbm, flags), (table_hbm, table)]
+        )
+    ]
+    order = []
     for chunk in reversed(range(chunks)):
         begin = max(0, chunk * CHUNK - lead)
         order += [f for f in range(begin, (chunk + 1) * CHUNK) if f not in order]
-    for frame in order:
+    for frame in order[:5]:
         load(frame).start()
-
-    barrier = pltpu.get_barrier_semaphore()
-    for d in offsets:
-        pl.semaphore_signal(
-            barrier, inc=1, device_id={"inp": lax.rem(me + d, peers)}, device_id_type=MESH
-        )
-    pl.semaphore_signal(barrier, inc=1, device_id={"tm": other}, device_id_type=MESH)
-    pl.semaphore_wait(barrier, peers)
+    for constant in constants:
+        constant.start()
+    for frame in order[5:]:
+        load(frame).start()
+    barrier_part(False)
 
     halo = pltpu.make_async_remote_copy(
         src_ref=halo_out, dst_ref=halo_in, send_sem=halo_sems.at[0], recv_sem=halo_sems.at[1],
         device_id={"tm": other}, device_id_type=MESH,
     )
-    for j in range(lead):
-        load(frames - lead + j).wait()
-        halo_out[j] = volts[frames + j].astype(jnp.float32).astype(jnp.bfloat16)
-    halo.start()
 
     def filter_pair(first):
         def row_group(g, carry):
@@ -111,8 +121,13 @@
     dims = (((1,), (1,)), ((), ()))
 
     def compute(chunk):
+        good = flags[0:1, :].astype(jnp.float32)
+
         def pair(q, carry):
             first = chunk * CHUNK + 2 * q
+            if chunk == chunks - 1:
+                load(first).wait()
+                load(first + 1).wait()
             filter_pair(first)
             both = lax.dot_general(
                 table[...], high[...], dims, preferred_element_type=jnp.float32
@@ -121,7 +136,6 @@
                 table[: 2 * CH], low[...], dims, preferred_element_type=jnp.float32
             )
             total = both[: 2 * CH] + (both[2 * CH :] + rest)
-            good = flags[0:1, :]
             for j in range(2):
                 spectra[pl.ds(pl.multiple_of((2 * q + j) * 2 * CH, 2 * CH), 2 * CH), :] = (
                     total[:, j * rows : (j + 1) * rows] * good
@@ -130,15 +144,19 @@
 
         lax.fori_loop(0, CHUNK // 2, pair, 0)
 
-        def regroup(step, carry):
-            for u in range(8):
-                r = step * 8 + u
-                ready[chunk, r] = spectra[pl.ds(r, CHUNK, stride=2 * CH), :].astype(
-                    jnp.bfloat16
-                )
+    def regroup(chunk, dest):
+        unroll = math.gcd(mine, 8)
+
+        def some(step, carry):
+            for u in range(unroll):
+                chan = dest * mine + step * unroll + u
+                parts = [
+                    spectra[pl.ds(2 * chan + p, CHUNK, stride=2 * CH), :] for p in range(2)
+                ]
+                ready[chunk, chan] = jnp.concatenate(parts, axis=0).astype(jnp.bfloat16)
             return carry
 
-        lax.fori_loop(0, 2 * CH // 8, regroup, 0)
+        lax.fori_loop(0, mine // unroll, some, 0)
 
     def to_peer(chunk, d):
         dest = lax.rem(me + d, peers)
@@ -172,22 +190,33 @@
             device_id={"tm": other}, device_id_type=MESH,
         )
 
-    waited = set(range(frames - lead, frames))
+    waited = set(range((chunks - 1) * CHUNK, frames))
     for chunk in reversed(range(chunks)):
         for f in range(max(0, chunk * CHUNK - lead), (chunk + 1) * CHUNK):
             if f not in waited:
                 waited.add(f)
                 load(f).wait()
+        if chunk == chunks - 1:
+            for constant in constants:
+                constant.wait()
         if chunk == 0:
             halo.wait()
             scale = core.astype(jnp.float32)
             for j in range(lead):
                 volts[j] = (halo_in[j].astype(jnp.float32) * scale).astype(jnp.int32)
         compute(chunk)
+        if chunk == chunks - 1:
+            barrier_part(True)
         for d in offsets:
+            regroup(chunk, lax.rem(me + d, peers))
             to_peer(chunk, d).start()
+        regroup(chunk, me)
         own_local(chunk).start()
         own_other(chunk).start()
+        if chunk == chunks - 1:
+            for j in range(lead):
+                halo_out[j] = volts[frames + j].astype(jnp.float32).astype(jnp.bfloat16)
+            halo.start()
 
     for chunk in reversed(range(chunks)):
         for d in offsets:
@@ -208,25 +237,29 @@
     lead = TAPS - 1
     window = jnp.asarray((window_table() / 128.0).astype(np.float32))
     table = jnp.asarray(split_table())
-    good = jnp.broadcast_to(flags.astype(jnp.float32)[None, :], (8, rows))
-    vmem = pl.BlockSpec(memory_space=pltpu.VMEM)
+    good = flags.reshape(1, rows)
+    stay = pl.BlockSpec(memory_space=pltpu.HBM)
     anywhere = pl.BlockSpec(memory_space=pl.ANY)
     return pl.pallas_call(
         functools.partial(spread_kernel, peers, frames),
         out_shape=jax.ShapeDtypeStruct(
-            (peers, 2, chunks, 2 * CH // peers, CHUNK, rows), jnp.bfloat16
+            (peers, 2, chunks, CH // peers, 2 * CHUNK, rows), jnp.bfloat16
         ),
-        in_specs=[anywhere, vmem, vmem, vmem],
+        in_specs=[stay, stay, stay, stay],
         out_specs=anywhere,
         scratch_shapes=[
             pltpu.VMEM((frames + lead, rows, NFFT), jnp.int32),
+            pltpu.VMEM((1, rows), jnp.int32),
+            pltpu.VMEM((TAPS, NFFT), jnp.float32),
+            pltpu.VMEM((4 * CH, NFFT), jnp.bfloat16),
             pltpu.VMEM((lead, rows, NFFT), jnp.bfloat16),
             pltpu.VMEM((lead, rows, NFFT), jnp.bfloat16),
             pltpu.VMEM((2 * rows, NFFT), jnp.bfloat16),
             pltpu.VMEM((2 * rows, NFFT), jnp.bfloat16),
             pltpu.VMEM((CHUNK * 2 * CH, rows), jnp.float32),
-            pltpu.VMEM((chunks, 2 * CH, CHUNK, rows), jnp.bfloat16),
+            pltpu.VMEM((chunks, CH, 2 * CHUNK, rows), jnp.bfloat16),
             pltpu.SemaphoreType.DMA((frames,)),
+            pltpu.SemaphoreType.DMA((3,)),
             pltpu.SemaphoreType.DMA((2,)),
             pltpu.SemaphoreType.DMA((chunks, peers)),
             pltpu.SemaphoreType.DMA((chunks, peers)),
@@ -244,52 +277,49 @@
 def correlate_kernel(block, out, left, right):
     peers, cores, chunks, _, length, rows = block.shape
     half = peers // 2
+    frames = length // 2
+    width = half * rows
     core = lax.axis_index("tm")
-    width = length * 2
-    for src in range(peers):
-        cols = slice(src * rows, (src + 1) * rows)
-        for t in range(cores):
-            for k in range(chunks):
-                at = (t * chunks + k) * width
-                real, imag = block[src, t, k, 0], block[src, t, k, 1]
-                left[0, at : at + length, cols] = real
-                left[0, at + length : at + width, cols] = imag
-                left[1, at : at + length, cols] = imag
-                left[1, at + length : at + width, cols] = -real
-    for s in range(half):
-        cols = slice(s * rows, (s + 1) * rows)
-        for t in range(cores):
-            for k in range(chunks):
-                at = (t * chunks + k) * width
-                right[at : at + length, cols] = block[core * half + s, t, k, 0]
-                right[at + length : at + width, cols] = block[core * half + s, t, k, 1]
+    for t in range(cores):
+        for k in range(chunks):
+            at = (t * chunks + k) * length
+            for src in range(peers):
+                left[at : at + length, src * rows : (src + 1) * rows] = block[src, t, k, 0]
+            for s in range(half):
+                tile = block[core * half + s, t, k, 0]
+                wide = tile.astype(jnp.float32)
+                turned = jnp.concatenate([-wide[frames:], wide[:frames]], axis=0)
+                right[at : at + length, s * rows : (s + 1) * rows] = tile
+                right[at : at + length, width + s * rows : width + (s + 1) * rows] = (
+                    turned.astype(jnp.bfloat16)
+                )
     step = 256
-    for r in range(2):
-        for a in range(0, left.shape[2], step):
-            out[0, r, a : a + step, :] = lax.dot_general(
-                left[r, :, a : a + step], right[...], (((0,), (0,)), ((), ())),
-                preferred_element_type=jnp.float32,
-            ).astype(jnp.bfloat16)
+    for a in range(0, left.shape[1], step):
+        both = lax.dot_general(
+            left[:, a : a + step], right[...], (((0,), (0,)), ((), ())),
+            preferred_element_type=jnp.float32,
+        ).astype(jnp.bfloat16)
+        out[0, 0, a : a + step, :] = both[:, :width]
+        out[0, 1, a : a + step, :] = both[:, width:]
 
 
 def correlate_blocks(gathered):
-    peers, cores, chunks, parts, length, rows = gathered.shape
-    chans = parts // 2
+    peers, cores, chunks, chans, length, rows = gathered.shape
     total = peers * rows
-    depth = cores * chunks * 2 * length
+    depth = cores * chunks * length
     return pl.pallas_call(
         correlate_kernel,
         grid=(chans,),
         out_shape=jax.ShapeDtypeStruct((chans, 2, total, total // 2), jnp.bfloat16),
         in_specs=[
             pl.BlockSpec(
-                (peers, cores, chunks, 2, length, rows), lambda c: (0, 0, 0, c, 0, 0)
+                (peers, cores, chunks, 1, length, rows), lambda c: (0, 0, 0, c, 0, 0)
             )
         ],
         out_specs=pl.BlockSpec((1, 2, total, total // 2), lambda c: (c, 0, 0, 0)),
         scratch_shapes=[
-            pltpu.VMEM((2, depth, total), jnp.bfloat16),
-            pltpu.VMEM((depth, total // 2), jnp.bfloat16),
+            pltpu.VMEM((depth, total), jnp.bfloat16),
+            pltpu.VMEM((depth, total), jnp.bfloat16),
         ],
         compiler_params=pltpu.CompilerParams(vmem_limit_bytes=48 << 20),
         name="correlate",

time: 84.9 us -> 78.3 us (0.922); the launches traced: 83.3 us -> 78 us
  Pallas kernels: 80.7 us -> 75.4 us
    pallas_call x1, Pallas kernels: 62.8 us -> 57.7 us  [spread(): pl.pallas_call(functools.partial(spread_kernel, peers, frames), out_shape...]
    unnamed x4 -> x6, local copies, waits for them, and re-layouts: 1.94 us -> 2.6 us
where the time goes in v2:
time: 78.3 us; the launch traced here: 78 us
  Pallas kernels  75.4 us (96%)
  local copies, waits for them, and re-layouts  2.6 us (3%)
    pallas_call x1, Pallas kernels, spread(): pl.pallas_call(functools.partial(spread_kernel, peers, frames), out_shape...  57.7 us
    pallas_call x1, Pallas kernels, correlate_blocks(): pl.pallas_call(correlate_kernel, grid=(chans,), out_shape=jax.ShapeDtypeS...  17.7 us
    unnamed x6, local copies, waits for them, and re-layouts  2.6 us

profile of v2, /device:TPU:0, one launch (start us, length us, event | category | flops | bytes accessed | tf_op | source)
XLA Modules:
  0.0 78.0 jit_solution(12762662214823831152)
XLA Ops:
  0.0 0.0 copy-start
  0.0 1.2 %copy-done = bf16[512,1024]{1,0:T(8,128)(2,1)S(1)} copy-done((bf16[512,1024]{1,0:T(8,128)(2,1)S(1)}, bf16[512,1024]{1,0:T(8,128)(2,1)}, u32[]{:S(2)}) %copy-start) | copy-done | bytes 1048600
  1.2 0.0 copy-start.1
  1.2 0.7 copy-done.1
  1.9 0.0 copy-start.2
  1.9 0.7 copy-done.2
  2.6 57.7 %filter_transform_spread.1.block = bf16[8,2,4,16,16,128]{5,4,3,2,1,0:T(8,128)(2,1)S(1)} custom-call(s32[128,32768]{1,0:T(8,128)} %samples.1, s32[1,128]{1,0:T(1,128)S(1)} %bitcast.1, f32[4,1024]{1,0:T(4,128)S(1)} %copy-done.1, bf16[512,1024]{1,0:T(8,128)(2,1)S(1)} %copy-done), custom_call_target="tpu_custom_call" | custom-call | tf_op jit(solution)/shard_map/filter_transform_spread/pallas_call | solution.py:243
  60.3 17.7 %correlate.1 = bf16[16,2,1024,512]{3,2,1,0:T(8,128)(2,1)} custom-call(bf16[8,2,4,16,16,128]{5,4,3,2,1,0:T(8,128)(2,1)S(1)} %filter_transform_spread.1.block), custom_call_target="tpu_custom_call" | custom-call | tf_op jit(solution)/shard_map/correlate/pallas_call | solution.py:310
Async XLA Ops:
  0.0 1.2 %copy-start = (bf16[512,1024]{1,0:T(8,128)(2,1)S(1)}, bf16[512,1024]{1,0:T(8,128)(2,1)}, u32[]{:S(2)}) copy-start(bf16[512,1024]{1,0:T(8,128)(2,1)} %constant.5.clone.table_hbm) | copy-start | bytes 3145732
  1.2 0.7 copy-start.1
  1.9 0.7 copy-start.2
